TPU v7x, 128 devices: a whole 4x4x4 slice. The times are simulated.
128 devices in a mesh: freq: 16 (over x, y), slab: 8 (over z, core).
Axes of the slice: x: 4, y: 4, z: 4, core: 2. Of those that a mesh axis runs over, the one named last changes fastest.
Arguments:
- fine_model: bfloat16 [2048, 2048], P(('freq', 'slab')), may hold values from 0.5 to 2
- resample: bfloat16 [16, 1024, 2048], P('freq', 'slab'), may hold values from -0.125 to 0.125
- lateral: bfloat16 [2048, 2048], replicated, may hold values from -0.0625 to 0.0625
- shift: float32 [16], P('freq'), may hold values from 0.5 to 4
- source: float32 [16, 1024, 2048], P('freq', 'slab'), may hold values from -6 to 6
- receiver: float32 [16, 1024, 2048], P('freq', 'slab'), may hold values from -6 to 6
Outputs:
- image: float32 [2048, 2048], P(('freq', 'slab'))
All inputs are finite; a program needn't handle non-finite values.
Results may differ from a plain program's by a relative error of at most 0.0029.
Values may be sent and summed in bfloat16 or wider, within the bound.
A program may use at most 128 MiB of HBM per device.

v0:
```python
import jax
import jax.numpy as jnp
from jax import lax
from jax.sharding import PartitionSpec as P

SWEEPS = 8
HALO = 8


def with_halo(value, size):
    up = [(i, i + 1) for i in range(size - 1)]
    down = [(i + 1, i) for i in range(size - 1)]
    before = lax.ppermute(value[-HALO:], "slab", up)
    after = lax.ppermute(value[:HALO], "slab", down)
    return jnp.concatenate([before, value, after], axis=0)


def shards(fine_model, resample, lateral, shift, source, receiver):
    freqs, slabs = (lax.axis_size("freq"), lax.axis_size("slab"))
    oper = resample[0]
    rows = oper.shape[0]
    every = lax.all_gather(oper, "slab", axis=0, tiled=True)
    wide = with_halo(oper, slabs)
    src = with_halo(source[0], slabs)
    model = lax.all_gather(fine_model, ("freq", "slab"), axis=0, tiled=True)
    coarse = jnp.dot(wide, model, preferred_element_type=jnp.float32)
    at = (
        lax.axis_index("slab") * rows
        - HALO
        + lax.broadcasted_iota(jnp.int32, (rows + 2 * HALO, 1), 0)
    )
    inside = (at >= 0) & (at < rows * slabs)
    inv = jnp.where(inside, 1.0 / (4.0 + shift[0] * coarse * coarse), 0.0)
    field = src * inv
    for sweep in range(1, SWEEPS):
        padded = jnp.pad(field, ((1, 1), (0, 0)))
        beside = padded[2:] + padded[:-2]
        side = jnp.dot(field.astype(jnp.bfloat16), lateral, preferred_element_type=jnp.float32)
        field = (src + 0.5 * beside + side) * inv
    part = (field[HALO:-HALO] * receiver[0]).astype(jnp.bfloat16)
    cols = lax.all_to_all(part, "slab", split_axis=1, concat_axis=0, tiled=True)
    term = lax.dot_general(
        every, cols, (((0,), (0,)), ((), ())), preferred_element_type=jnp.float32
    )
    mine = lax.psum_scatter(term, "freq", scatter_dimension=0, tiled=True)
    return lax.all_to_all(mine, "slab", split_axis=0, concat_axis=1, tiled=True)


def solution(mesh):
    in_specs = (
        P(("freq", "slab"), None),
        P("freq", "slab", None),
        P(),
        P("freq"),
        P("freq", "slab", None),
        P("freq", "slab", None),
    )
    out_specs = P(("freq", "slab"), None)
    return jax.shard_map(shards, mesh=mesh, in_specs=in_specs, out_specs=out_specs, check_vma=False)
```

profile of v0, /device:TPU:1, one launch (start us, length us, event | category | flops | bytes accessed | tf_op | source)
XLA Modules:
  0.0 218.3 jit_solution(8704276760987448156)
XLA Ops:
  6.5 0.7 all-gather.4.cloned.1.call-update
  7.3 0.0 all-gather.6.cloned.1.call-start
  7.3 0.9 slice_bitcast_fusion.1
  8.2 4.9 %collective-permute-start = (f32[8,2048]{1,0:T(8,128)S(1)}, f32[8,2048]{1,0:T(8,128)S(1)}, u32[]{:S(2)}, u32[]{:S(2)}) collective-permute-start(f32[8,2048]{1,0:T(8,128)S(1)} %get-tuple-element.9), channel_id=1, source_target_pairs={{0,1},{1,2},{2,3},{3,4},{4,5},{5,6},{6,7},{8,9},{9,10},{10,11},{11... | collective-permute-start | bytes 196616 | tf_op jit(solution)/shard_map/ppermute | solution.py:13
  13.1 1.9 collective-permute-start.1
  15.1 0.0 all-gather.6.cloned.1.call-update
  15.1 0.8 slice_bitcast_fusion.3
  15.9 3.6 %collective-permute-start.2 = (bf16[8,2048]{1,0:T(8,128)(2,1)S(1)}, bf16[8,2048]{1,0:T(8,128)(2,1)S(1)}, u32[]{:S(2)}, u32[]{:S(2)}) collective-permute-start(bf16[8,2048]{1,0:T(8,128)(2,1)S(1)} %get-tuple-element.11), channel_id=1, source_target_pairs={{0,1},{1,2},{2,3},{3,4},{4,5},{5,6},{6,7},{8,9},{9,10},{10,11},{11... | collective-permute-start | bytes 98312 | tf_op jit(solution)/shard_map/ppermute | solution.py:13
  19.5 1.9 collective-permute-start.3
  22.1 2.6 %collective-permute-done.3 = bf16[8,2048]{1,0:T(8,128)(2,1)S(1)} collective-permute-done((bf16[8,2048]{1,0:T(8,128)(2,1)S(1)}, bf16[8,2048]{1,0:T(8,128)(2,1)S(1)}, u32[]{:S(2)}, u32[]{:S(2)}) %collective-permute-start.3) | collective-permute-done | bytes 32800 | tf_op jit(solution)/shard_map/ppermute | solution.py:14
  24.7 59.4 %all-gather.4.cloned.1.call-done = bf16[2048,2048]{1,0:T(8,128)(2,1)} async-done(((bf16[16,2048]{1,0:T(8,128)(2,1)}), bf16[2048,2048]{1,0:T(8,128)(2,1)}) %all-gather.4.cloned.1.call-update) | async-done | bytes 8388624 | tf_op jit(solution)/shard_map/all_gather | solution.py:25
  84.1 5.5 %pad_maximum_fusion = (f32[144,2048]{1,0:T(8,128)S(1)}, f32[144,2048]{1,0:T(8,128)S(1)}, f32[144,2048]{1,0:T(8,128)S(1)}) fusion(f32[8,2048]{1,0:T(8,128)S(1)} %collective-permute-done.1, f32[128,2048]{1,0:T(8,128)} %bitcast.43, f32[8,2048]{1,0:T(8,128)S(1)} %collective-permute-done, bf16[2048,2048]{1,0:T(8,128)(2,1)} %all-gather.4.cloned.1.call-done, ...), kind=kOutput, calls=%fused_computation.51 | convolution fusion | flops 1212088320 | bytes 13697172 | tf_op jit(solution)/shard_map/dot_general | solution.py:26
  89.6 0.8 slice-done.1
  90.4 0.2 copy-done
  90.7 1.6 fusion.9
  92.3 1.6 fusion.14
  93.9 1.6 fusion.19
  95.5 1.6 fusion.24
  97.1 1.6 fusion.29
  98.7 1.6 fusion.34
  100.3 0.4 pad_slice_fusion.1
  100.7 1.4 fusion.49
  102.1 0.6 fusion.39
  102.7 0.8 copy.16
  103.5 3.7 %all-to-all-start = ((bf16[128,8,256]{2,0,1:T(8,128)(2,1)}), bf16[128,8,256]{2,0,1:T(8,128)(2,1)S(1)}, u32[]{:S(2)}, u32[]{:S(2)}) async-start(bf16[128,8,256]{2,0,1:T(8,128)(2,1)} %bitcast.39), calls=%async_computation | async-start | bytes 1048576 | tf_op jit(solution)/shard_map/all_to_all | solution.py:41
  107.2 12.3 %all-gather.6.cloned.1.call-done = bf16[1,1024,2048]{2,1,0:T(8,128)(2,1)} async-done(((bf16[1,128,2048]{2,1,0:T(8,128)(2,1)}), bf16[1,1024,2048]{2,1,0:T(8,128)(2,1)}) %all-gather.6.cloned.1.call-update) | async-done | bytes 4194320 | tf_op jit(solution)/shard_map/all_gather | solution.py:22
  119.4 0.1 all-to-all-done
  119.6 4.8 %fusion.2 = f32[2048,256]{0,1:T(8,128)} fusion(bf16[1024,256]{1,0:T(8,128)(2,1)S(1)} %bitcast.52, bf16[1,1024,2048]{2,1,0:T(8,128)(2,1)} %all-gather.6.cloned.1.call-done), kind=kOutput, calls=%fused_computation.2 | convolution fusion | flops 1073741824 | bytes 6815744 | tf_op jit(solution)/shard_map/dot_general | solution.py:42
  124.4 73.9 %reduce-scatter.2.cloned.1.call-done = f32[128,256]{0,1:T(8,128)} async-done(((f32[2048,256]{0,1:T(8,128)}), f32[128,256]{0,1:T(8,128)}) %reduce-scatter.2.cloned.1.call-update) | async-done | bytes 131088 | tf_op jit(solution)/shard_map/reduce_scatter | solution.py:45
  198.3 1.0 copy.11
  199.3 11.9 %all_to_all.38 = f32[8,16,256]{2,1,0:T(8,128)S(1)} all-to-all(f32[8,16,256]{2,1,0:T(8,128)S(1)} %bitcast.53), channel_id=1, replica_groups=mesh['freq'=16,'slab'=8] {'slab'}, dimensions={0} | all-to-all | bytes 262144 | tf_op jit(solution)/shard_map/all_to_all | solution.py:46
  211.1 0.7 copy.14
  (14 shorter events, 0.0 us)
Async XLA Ops:
  6.5 77.6 %all-gather.4.cloned.1.call-start = ((), (), s32[]{:S(2)}) async-start(), calls=%async_computation.3 | async-start | bytes 8454144 | tf_op jit(solution)/shard_map/all_gather | solution.py:25
  7.3 112.2 %all-gather.6.cloned.1.call-start = ((), (), s32[]{:S(2)}) async-start(), calls=%async_computation.5 | async-start | bytes 4718592 | tf_op jit(solution)/shard_map/all_gather | solution.py:22
  8.2 16.6 %collective-permute-start = (f32[8,2048]{1,0:T(8,128)S(1)}, f32[8,2048]{1,0:T(8,128)S(1)}, u32[]{:S(2)}, u32[]{:S(2)}) collective-permute-start(f32[8,2048]{1,0:T(8,128)S(1)} %get-tuple-element.9), channel_id=1, source_target_pairs={{0,1},{1,2},{2,3},{3,4},{4,5},{5,6},{6,7},{8,9},{9,10},{10,11},{11... | collective-permute-start | bytes 196616 | tf_op jit(solution)/shard_map/ppermute | solution.py:13
  13.1 11.6 %collective-permute-start.1 = (f32[8,2048]{1,0:T(8,128)S(1)}, f32[8,2048]{1,0:T(8,128)S(1)}, u32[]{:S(2)}, u32[]{:S(2)}) collective-permute-start(f32[8,2048]{1,0:T(8,128)S(1)} %get-tuple-element.10), channel_id=1, source_target_pairs={{1,0},{2,1},{3,2},{4,3},{5,4},{6,5},{7,6},{9,8},{10,9},{11,10},{12... | collective-permute-start | bytes 196616 | tf_op jit(solution)/shard_map/ppermute | solution.py:14
  15.9 6.2 %collective-permute-start.2 = (bf16[8,2048]{1,0:T(8,128)(2,1)S(1)}, bf16[8,2048]{1,0:T(8,128)(2,1)S(1)}, u32[]{:S(2)}, u32[]{:S(2)}) collective-permute-start(bf16[8,2048]{1,0:T(8,128)(2,1)S(1)} %get-tuple-element.11), channel_id=1, source_target_pairs={{0,1},{1,2},{2,3},{3,4},{4,5},{5,6},{6,7},{8,9},{9,10},{10,11},{11... | collective-permute-start | bytes 98312 | tf_op jit(solution)/shard_map/ppermute | solution.py:13
  19.5 5.2 %collective-permute-start.3 = (bf16[8,2048]{1,0:T(8,128)(2,1)S(1)}, bf16[8,2048]{1,0:T(8,128)(2,1)S(1)}, u32[]{:S(2)}, u32[]{:S(2)}) collective-permute-start(bf16[8,2048]{1,0:T(8,128)(2,1)S(1)} %get-tuple-element.12), channel_id=1, source_target_pairs={{1,0},{2,1},{3,2},{4,3},{5,4},{6,5},{7,6},{9,8},{10,9},{11,10},{12... | collective-permute-start | bytes 98312 | tf_op jit(solution)/shard_map/ppermute | solution.py:14
  84.1 5.5 %slice-start = ((s8[8388608]{0:T(1024)(128)(4,1)}), s8[4194304]{0:T(1024)(128)(4,1)S(1)}, s32[]{:S(2)}) async-start(s8[8388608]{0:T(1024)(128)(4,1)} %bitcast.41), calls=%async_computation.6 | async-start | bytes 8388608
  84.1 6.3 %slice-start.1 = ((s8[8388608]{0:T(1024)(128)(4,1)}), s8[4194304]{0:T(1024)(128)(4,1)S(1)}, s32[]{:S(2)}) async-start(s8[8388608]{0:T(1024)(128)(4,1)} %bitcast.41), calls=%async_computation.7 | async-start | bytes 8388608
  84.1 6.5 %copy-start = (f32[1,128,2048]{2,1,0:T(8,128)S(1)}, f32[1,128,2048]{2,1,0:T(8,128)}, u32[]{:S(2)}) copy-start(f32[1,128,2048]{2,1,0:T(8,128)} %param.10) | copy-start | bytes 3145732
  100.6 1.4 copy-start.1
  103.5 16.1 %all-to-all-start = ((bf16[128,8,256]{2,0,1:T(8,128)(2,1)}), bf16[128,8,256]{2,0,1:T(8,128)(2,1)S(1)}, u32[]{:S(2)}, u32[]{:S(2)}) async-start(bf16[128,8,256]{2,0,1:T(8,128)(2,1)} %bitcast.39), calls=%async_computation | async-start | bytes 1048576 | tf_op jit(solution)/shard_map/all_to_all | solution.py:41
  107.2 91.1 %reduce-scatter.2.cloned.1.call-start = ((), (), s32[]{:S(2)}) async-start(), calls=%async_computation.4 | async-start | bytes 2228224 | tf_op jit(solution)/shard_map/reduce_scatter | solution.py:45
Sparse Core Ops, SparseCore 0:
  10.3 73.7 all-gather.3
  85.8 33.5 all-gather.5
  124.5 73.7 reduce-scatter.1
where the time goes:
time: 219 us; the launch traced here: 218 us
  waiting for transfers between devices  149 us (68%)
  matrix products  21.2 us (10%)
  starting transfers between devices  16.1 us (7%)
  between operations  13.9 us (6%)
  blocking collectives  11.9 us (5%)
  local copies, waits for them, and re-layouts  5.6 us (3%)
    reduce_scatter x1, waiting for transfers between devices, shards(): mine = lax.psum_scatter(term, 'freq', scatter_dimension=0, tiled=True)  73.9 us
    all_gather x1, waiting for transfers between devices, shards(): model = lax.all_gather(fine_model, ('freq', 'slab'), axis=0, tiled=True)  59.4 us
    all_gather x1, waiting for transfers between devices, shards(): every = lax.all_gather(oper, 'slab', axis=0, tiled=True)  12.3 us
    all_to_all x1, blocking collectives, shards(): return lax.all_to_all(mine, 'slab', split_axis=0, concat_axis=1, tiled=True)  11.9 us
    dot_general x7, matrix products, shards(): jnp.dot(field.astype(jnp.bfloat16), lateral, preferred_element_type=jnp.f...  10.9 us
    ppermute x2, starting transfers between devices, with_halo(): before = lax.ppermute(value[-HALO:], 'slab', up)  8.57 us
    dot_general x1, matrix products, shards(): coarse = jnp.dot(wide, model, preferred_element_type=jnp.float32)  5.46 us
    dot_general x1, matrix products, shards(): lax.dot_general(every, cols, (((0,), (0,)), ((), ())), preferred_element_...  4.78 us
  transfers between devices with their start and end apart: 8, of which 5 were waited for; matrix products, arithmetic and copies ran while one was open for 9% of the time, Pallas kernels for 0%

commit v1 on v0

--- a/solution.py
+++ b/solution.py
@@ -22,7 +22,12 @@
     every = lax.all_gather(oper, "slab", axis=0, tiled=True)
     wide = with_halo(oper, slabs)
     src = with_halo(source[0], slabs)
-    model = lax.all_gather(fine_model, ("freq", "slab"), axis=0, tiled=True)
+    model = jnp.concatenate(
+        lax.all_to_all(
+            jnp.stack([fine_model] * lax.axis_size(("freq", "slab"))), ("freq", "slab"), 0, 0
+        ),
+        axis=0,
+    )
     coarse = jnp.dot(wide, model, preferred_element_type=jnp.float32)
     at = (
         lax.axis_index("slab") * rows

time: 219 us -> 259 us (1.18)
  waiting for transfers between devices: 149 us -> 171 us
  starting transfers between devices: 16.1 us -> 30.7 us
  local copies, waits for them, and re-layouts: 5.6 us -> 8.87 us
    ppermute x2, waiting for transfers between devices: 2.63 us -> 89.3 us  [with_halo(): after = lax.ppermute(value[:HALO], 'slab', down)]
    all_gather x1 -> x0, waiting for transfers between devices: 59.4 us -> none  [shards(): model = lax.all_gather(fine_model, ('freq', 'slab'), axis=0, tiled=True)]
    all_gather x1, waiting for transfers between devices: 12.3 us -> 0.01 us  [shards(): every = lax.all_gather(oper, 'slab', axis=0, tiled=True)]
    all_to_all x0 -> x1, starting transfers between devices: none -> 12 us  [shards(): lax.all_to_all(jnp.stack([fine_model] * lax.axis_size(('freq', 'slab'))),...]
    all_to_all x1, waiting for transfers between devices: 0.14 us -> 9.48 us  [shards(): cols = lax.all_to_all(part, 'slab', split_axis=1, concat_axis=0, tiled=True)]
    another operation x0 -> x1, local copies, waits for them, and re-layouts: none -> 5.12 us  [shards(): jnp.stack([fine_model] * lax.axis_size(('freq', 'slab')))]
    all_to_all x1, starting transfers between devices: 3.65 us -> 7.52 us  [shards(): cols = lax.all_to_all(part, 'slab', split_axis=1, concat_axis=0, tiled=True)]
    reduce_scatter x1, waiting for transfers between devices: 73.9 us -> 70.9 us  [shards(): mine = lax.psum_scatter(term, 'freq', scatter_dimension=0, tiled=True)]
  transfers between devices with their start and end apart: 8 -> 8, of which waited for: 5 -> 4; matrix products, arithmetic and copies ran while one was open for 9% -> 7% of each run, Pallas kernels for 0% -> 0%
where the time goes in v1:
time: 259 us; the launch traced here: 258 us
  waiting for transfers between devices  171 us (66%)
  starting transfers between devices  30.7 us (12%)
  matrix products  20.9 us (8%)
  between operations  14.2 us (5%)
  blocking collectives  11.8 us (5%)
  local copies, waits for them, and re-layouts  8.87 us (3%)
    ppermute x2, waiting for transfers between devices, with_halo(): after = lax.ppermute(value[:HALO], 'slab', down)  89.3 us
    reduce_scatter x1, waiting for transfers between devices, shards(): mine = lax.psum_scatter(term, 'freq', scatter_dimension=0, tiled=True)  70.9 us
    all_to_all x1, starting transfers between devices, shards(): lax.all_to_all(jnp.stack([fine_model] * lax.axis_size(('freq', 'slab'))),...  12 us
    all_to_all x1, blocking collectives, shards(): return lax.all_to_all(mine, 'slab', split_axis=0, concat_axis=1, tiled=True)  11.8 us
    dot_general x7, matrix products, shards(): jnp.dot(field.astype(jnp.bfloat16), lateral, preferred_element_type=jnp.f...  10.9 us
    all_to_all x1, waiting for transfers between devices, shards(): cols = lax.all_to_all(part, 'slab', split_axis=1, concat_axis=0, tiled=True)  9.48 us
    all_to_all x1, starting transfers between devices, shards(): cols = lax.all_to_all(part, 'slab', split_axis=1, concat_axis=0, tiled=True)  7.52 us
    ppermute x2, starting transfers between devices, with_halo(): before = lax.ppermute(value[-HALO:], 'slab', up)  6.17 us
  transfers between devices with their start and end apart: 8, of which 4 were waited for; matrix products, arithmetic and copies ran while one was open for 7% of the time, Pallas kernels for 0%

profile of v1, /device:TPU:1, one launch (start us, length us, event | category | flops | bytes accessed | tf_op | source)
XLA Modules:
  0.0 258.2 jit_solution(5672706888894112103)
XLA Ops:
  6.5 5.1 %stack.2 = bf16[128,16,2048]{2,1,0:T(8,128)(2,1)} broadcast(bf16[16,2048]{1,0:T(8,128)(2,1)} %param.6), dimensions={1,2} | broadcast | bytes 8454144 | tf_op jit(solution)/shard_map/stack | solution.py:27
  11.7 12.0 %all-to-all-start = ((bf16[128,16,2048]{2,1,0:T(8,128)(2,1)}), bf16[128,16,2048]{2,1,0:T(8,128)(2,1)}, u32[]{:S(2)}, u32[]{:S(2)}) async-start(bf16[128,16,2048]{2,1,0:T(8,128)(2,1)} %stack.2), calls=%async_computation | async-start | bytes 16777216 | tf_op jit(solution)/shard_map/all_to_all | solution.py:26
  23.6 0.0 all-gather.3.cloned.1.call-start
  23.7 3.0 %collective-permute-start.1 = (f32[8,2048]{1,0:T(8,128)S(1)}, f32[8,2048]{1,0:T(8,128)S(1)}, u32[]{:S(2)}, u32[]{:S(2)}) collective-permute-start(f32[8,2048]{1,0:T(8,128)S(1)} %get-tuple-element.10), channel_id=1, source_target_pairs={{1,0},{2,1},{3,2},{4,3},{5,4},{6,5},{7,6},{9,8},{10,9},{11,10},{12... | collective-permute-start | bytes 196616 | tf_op jit(solution)/shard_map/ppermute | solution.py:14
  26.8 2.5 collective-permute-start
  29.3 0.0 all-gather.3.cloned.1.call-update
  29.3 1.9 collective-permute-start.3
  31.3 3.6 %collective-permute-start.2 = (bf16[8,2048]{1,0:T(8,128)(2,1)S(1)}, bf16[8,2048]{1,0:T(8,128)(2,1)S(1)}, u32[]{:S(2)}, u32[]{:S(2)}) collective-permute-start(bf16[8,2048]{1,0:T(8,128)(2,1)S(1)} %get-tuple-element.11), channel_id=1, source_target_pairs={{0,1},{1,2},{2,3},{3,4},{4,5},{5,6},{6,7},{8,9},{9,10},{10,11},{11... | collective-permute-start | bytes 98312 | tf_op jit(solution)/shard_map/ppermute | solution.py:13
  35.6 89.3 %collective-permute-done.3 = bf16[8,2048]{1,0:T(8,128)(2,1)S(1)} collective-permute-done((bf16[8,2048]{1,0:T(8,128)(2,1)S(1)}, bf16[8,2048]{1,0:T(8,128)(2,1)S(1)}, u32[]{:S(2)}, u32[]{:S(2)}) %collective-permute-start.3) | collective-permute-done | bytes 32800 | tf_op jit(solution)/shard_map/ppermute | solution.py:14
  124.9 0.0 collective-permute-done.1
  124.9 1.3 all-to-all-done
  126.2 5.2 %pad_maximum_fusion = (f32[144,2048]{1,0:T(8,128)S(1)}, f32[144,2048]{1,0:T(8,128)S(1)}, f32[144,2048]{1,0:T(8,128)S(1)}) fusion(f32[8,2048]{1,0:T(8,128)S(1)} %collective-permute-done.1, f32[128,2048]{1,0:T(8,128)S(1)} %bitcast.44, f32[8,2048]{1,0:T(8,128)S(1)} %collective-permute-done, bf16[2048,2048]{1,0:T(8,128)(2,1)} %bitcast.7, ...), kind=kOutput, calls=%fused_computation.51 | convolution fusion | flops 1212088320 | bytes 13697172 | tf_op jit(solution)/shard_map/dot_general | solution.py:31
  131.4 0.8 slice-done.1
  132.2 1.6 fusion.9
  133.8 1.6 fusion.14
  135.4 1.6 fusion.19
  137.0 1.6 fusion.24
  138.6 1.6 fusion.29
  140.2 1.6 fusion.34
  141.8 0.4 pad_slice_fusion.1
  142.2 0.0 copy-start.1
  142.2 1.4 fusion.49
  143.6 0.6 fusion.39
  144.3 0.8 copy.16
  145.1 7.5 %all-to-all-start.1 = ((bf16[128,8,256]{2,0,1:T(8,128)(2,1)}), bf16[128,8,256]{2,0,1:T(8,128)(2,1)S(1)}, u32[]{:S(2)}, u32[]{:S(2)}) async-start(bf16[128,8,256]{2,0,1:T(8,128)(2,1)} %bitcast.40), calls=%async_computation.1 | async-start | bytes 1048576 | tf_op jit(solution)/shard_map/all_to_all | solution.py:46
  152.6 9.5 %all-to-all-done.1 = bf16[128,8,256]{2,0,1:T(8,128)(2,1)S(1)} async-done(((bf16[128,8,256]{2,0,1:T(8,128)(2,1)}), bf16[128,8,256]{2,0,1:T(8,128)(2,1)S(1)}, u32[]{:S(2)}, u32[]{:S(2)}) %all-to-all-start.1) | async-done | bytes 524320 | tf_op jit(solution)/shard_map/all_to_all | solution.py:46
  162.1 4.8 %fusion.2 = f32[2048,256]{0,1:T(8,128)} fusion(bf16[1024,256]{1,0:T(8,128)(2,1)S(1)} %bitcast.53, bf16[1,1024,2048]{2,1,0:T(8,128)(2,1)} %all-gather.3.cloned.1.call-done), kind=kOutput, calls=%fused_computation.2 | convolution fusion | flops 1073741824 | bytes 6815744 | tf_op jit(solution)/shard_map/dot_general | solution.py:47
  166.9 0.0 reduce-scatter.2.cloned.1.call-update
  166.9 70.9 %reduce-scatter.2.cloned.1.call-done = f32[128,256]{0,1:T(8,128)} async-done(((f32[2048,256]{0,1:T(8,128)}), f32[128,256]{0,1:T(8,128)}) %reduce-scatter.2.cloned.1.call-update) | async-done | bytes 131088 | tf_op jit(solution)/shard_map/reduce_scatter | solution.py:50
  237.9 1.0 copy.11
  238.9 11.8 %all_to_all.43 = f32[8,16,256]{2,1,0:T(8,128)S(1)} all-to-all(f32[8,16,256]{2,1,0:T(8,128)S(1)} %bitcast.54), channel_id=1, replica_groups=mesh['freq'=16,'slab'=8] {'slab'}, dimensions={0} | all-to-all | bytes 262144 | tf_op jit(solution)/shard_map/all_to_all | solution.py:51
  250.7 0.7 copy.14
  (16 shorter events, 0.0 us)
Async XLA Ops:
  11.7 12.0 %copy-start = (f32[1,128,2048]{2,1,0:T(8,128)S(1)}, f32[1,128,2048]{2,1,0:T(8,128)}, u32[]{:S(2)}) copy-start(f32[1,128,2048]{2,1,0:T(8,128)} %param.10) | copy-start | bytes 3145732
  11.7 17.7 %copy-start.2 = (bf16[1,128,2048]{2,1,0:T(8,128)(2,1)S(1)}, bf16[1,128,2048]{2,1,0:T(8,128)(2,1)}, u32[]{:S(2)}) copy-start(bf16[1,128,2048]{2,1,0:T(8,128)(2,1)} %param.7) | copy-start | bytes 1572868
  11.7 114.6 %all-to-all-start = ((bf16[128,16,2048]{2,1,0:T(8,128)(2,1)}), bf16[128,16,2048]{2,1,0:T(8,128)(2,1)}, u32[]{:S(2)}, u32[]{:S(2)}) async-start(bf16[128,16,2048]{2,1,0:T(8,128)(2,1)} %stack.2), calls=%async_computation | async-start | bytes 16777216 | tf_op jit(solution)/shard_map/all_to_all | solution.py:26
  23.6 129.0 %all-gather.3.cloned.1.call-start = ((), (), s32[]{:S(2)}) async-start(), calls=%async_computation.5 | async-start | bytes 4718592 | tf_op jit(solution)/shard_map/all_gather | solution.py:22
  23.7 101.2 %collective-permute-start.1 = (f32[8,2048]{1,0:T(8,128)S(1)}, f32[8,2048]{1,0:T(8,128)S(1)}, u32[]{:S(2)}, u32[]{:S(2)}) collective-permute-start(f32[8,2048]{1,0:T(8,128)S(1)} %get-tuple-element.10), channel_id=1, source_target_pairs={{1,0},{2,1},{3,2},{4,3},{5,4},{6,5},{7,6},{9,8},{10,9},{11,10},{12... | collective-permute-start | bytes 196616 | tf_op jit(solution)/shard_map/ppermute | solution.py:14
  26.8 98.1 %collective-permute-start = (f32[8,2048]{1,0:T(8,128)S(1)}, f32[8,2048]{1,0:T(8,128)S(1)}, u32[]{:S(2)}, u32[]{:S(2)}) collective-permute-start(f32[8,2048]{1,0:T(8,128)S(1)} %get-tuple-element.9), channel_id=1, source_target_pairs={{0,1},{1,2},{2,3},{3,4},{4,5},{5,6},{6,7},{8,9},{9,10},{10,11},{11... | collective-permute-start | bytes 196616 | tf_op jit(solution)/shard_map/ppermute | solution.py:13
  29.3 95.5 %collective-permute-start.3 = (bf16[8,2048]{1,0:T(8,128)(2,1)S(1)}, bf16[8,2048]{1,0:T(8,128)(2,1)S(1)}, u32[]{:S(2)}, u32[]{:S(2)}) collective-permute-start(bf16[8,2048]{1,0:T(8,128)(2,1)S(1)} %get-tuple-element.12), channel_id=1, source_target_pairs={{1,0},{2,1},{3,2},{4,3},{5,4},{6,5},{7,6},{9,8},{10,9},{11,10},{12... | collective-permute-start | bytes 98312 | tf_op jit(solution)/shard_map/ppermute | solution.py:14
  31.3 93.6 %collective-permute-start.2 = (bf16[8,2048]{1,0:T(8,128)(2,1)S(1)}, bf16[8,2048]{1,0:T(8,128)(2,1)S(1)}, u32[]{:S(2)}, u32[]{:S(2)}) collective-permute-start(bf16[8,2048]{1,0:T(8,128)(2,1)S(1)} %get-tuple-element.11), channel_id=1, source_target_pairs={{0,1},{1,2},{2,3},{3,4},{4,5},{5,6},{6,7},{8,9},{9,10},{10,11},{11... | collective-permute-start | bytes 98312 | tf_op jit(solution)/shard_map/ppermute | solution.py:13
  126.2 5.2 %slice-start = ((s8[8388608]{0:T(1024)(128)(4,1)}), s8[4194304]{0:T(1024)(128)(4,1)S(1)}, s32[]{:S(2)}) async-start(s8[8388608]{0:T(1024)(128)(4,1)} %bitcast.42), calls=%async_computation.6 | async-start | bytes 8388608
  126.2 6.0 %slice-start.1 = ((s8[8388608]{0:T(1024)(128)(4,1)}), s8[4194304]{0:T(1024)(128)(4,1)S(1)}, s32[]{:S(2)}) async-start(s8[8388608]{0:T(1024)(128)(4,1)} %bitcast.42), calls=%async_computation.7 | async-start | bytes 8388608
  142.2 1.4 copy-start.1
  145.1 17.0 %all-to-all-start.1 = ((bf16[128,8,256]{2,0,1:T(8,128)(2,1)}), bf16[128,8,256]{2,0,1:T(8,128)(2,1)S(1)}, u32[]{:S(2)}, u32[]{:S(2)}) async-start(bf16[128,8,256]{2,0,1:T(8,128)(2,1)} %bitcast.40), calls=%async_computation.1 | async-start | bytes 1048576 | tf_op jit(solution)/shard_map/all_to_all | solution.py:46
  152.6 85.2 %reduce-scatter.2.cloned.1.call-start = ((), (), s32[]{:S(2)}) async-start(), calls=%async_computation.4 | async-start | bytes 2228224 | tf_op jit(solution)/shard_map/reduce_scatter | solution.py:50
Sparse Core Ops, SparseCore 0:
  29.4 110.1 all-gather.2
  167.0 70.7 reduce-scatter.1
